TPU v7x, 256 devices: a whole 4x4x8 slice. The times are simulated.
256 devices in a mesh: basis: 32 (over z_lo, y, core), state: 8 (over x, z_hi).
Axes of the slice: x: 4, y: 4, z: 8 (z_hi: 2, z_lo: 4; z = z_hi * 4 + z_lo), core: 2. Of those that a mesh axis runs over, the one named last changes fastest.
Arguments:
- vectors: bfloat16 [512, 163840], P('state', 'basis'), may hold values from -6 to 6
- blocks: bfloat16 [1280, 72, 128, 128], P('basis', 'state'), may hold values from -0.0625 to 0.0625
- columns: int32 [1280, 72], P('basis', 'state'), may hold values from 0 to 1279, as said below
- counts: int32 [1280], P('basis'), may hold values from 18 to 72, as said below
Outputs:
- sigma: bfloat16 [512, 163840], P('state', 'basis')
Inputs may be any that keep to these rules, and one draw needn't show every extreme that they name: Every block column lies within 36 blocks of its block row and inside the basis; a row's slots name distinct columns except near the basis ends, where a column may repeat. Slots k < counts[r] are live; some block row has all 72 slots live.
All inputs are finite; a program needn't handle non-finite values.
Results may differ from a plain program's by a relative error of at most 0.001.
Values may be sent and summed in bfloat16 or wider, within the bound.
A program may use at most 192 MiB of HBM per device.

v0:
```python
import jax
import jax.numpy as jnp
from jax import lax
from jax.sharding import PartitionSpec as P

W = 36


def extended(shard, sides, width):
    for axis, dim in sides:
        size, length = (lax.axis_size(axis), shard.shape[dim])
        up = [(i, (i + 1) % size) for i in range(size - 1)]
        down = [(j, i) for i, j in up]
        last = lax.slice_in_dim(shard, length - width, length, axis=dim)
        leading = lax.slice_in_dim(shard, 0, width, axis=dim)
        before = lax.ppermute(last, axis, up)
        after = lax.ppermute(leading, axis, down)
        shard = jnp.concatenate([before, shard, after], axis=dim)
    return shard


def on_device(vectors, blocks, columns, counts):
    shard_rows = vectors.shape[1]
    row_blocks = blocks.shape[0]
    own_slots = blocks.shape[1]
    block_size = blocks.shape[2]
    reach = W * block_size
    banded = extended(vectors, (("basis", 1),), reach)
    gathered = lax.all_gather(banded, "state", axis=0, tiled=True)
    first_block = lax.axis_index("basis") * row_blocks - W
    relative = (columns - first_block).reshape(-1)
    slot_index = lax.axis_index("state") * own_slots + jnp.arange(own_slots, dtype=jnp.int32)
    live_mask = (slot_index[None, :] < counts[:, None]).astype(jnp.bfloat16)
    row_count = vectors.shape[0] * lax.axis_size("state")
    state_part = gathered
    state_part = state_part.reshape(row_count, row_blocks + 2 * W, block_size)
    picked = jnp.take(state_part, relative, axis=1).reshape(
        row_count, row_blocks, own_slots, block_size
    )
    picked = picked * live_mask[None, :, :, None]
    result = jnp.einsum("srjb,rjcb->src", picked, blocks, preferred_element_type=jnp.float32)
    sigma_shard = lax.psum_scatter(
        result.reshape(row_count, shard_rows), "state", scatter_dimension=0, tiled=True
    )
    return sigma_shard.astype(jnp.bfloat16)


def solution(mesh):
    in_specs = (
        P("state", "basis"),
        P("basis", "state", None, None),
        P("basis", "state"),
        P("basis"),
    )
    out_specs = P("state", "basis")
    return jax.shard_map(
        on_device, mesh=mesh, in_specs=in_specs, out_specs=out_specs, check_vma=False
    )
```

profile of v0, /device:TPU:25, one launch (start us, length us, event | category | flops | bytes accessed | tf_op | source)
XLA Modules:
  0.0 622.3 jit_solution(12525188134928636910)
XLA Ops:
  6.5 0.0 all-gather.2.cloned.1.call-start
  6.5 1.4 fusion.8
  7.9 3.8 collective-permute-start
  11.7 1.9 collective-permute-start.1
  13.6 4.9 collective-permute-done
  18.5 6.5 %collective-permute-done.1 = bf16[64,4608]{1,0:T(8,128)(2,1)S(1)} collective-permute-done((bf16[64,4608]{1,0:T(8,128)(2,1)S(1)}, bf16[64,4608]{1,0:T(8,128)(2,1)S(1)}, u32[]{:S(2)}, u32[]{:S(2)}) %collective-permute-start.1) | collective-permute-done | bytes 589856 | tf_op jit(solution)/shard_map/ppermute | solution.py:17
  25.0 2.4 pad_maximum_fusion
  27.5 0.0 all-gather.2.cloned.1.call-update
  27.5 0.0 reduce-scatter.2.cloned.1.call-start
  27.5 0.7 compare_and_fusion
  28.2 0.1 copy.20
  28.3 0.1 reshape.82
  28.4 0.1 copy.18
  28.6 0.7 compare_convert_fusion
  29.3 272.9 %all-gather.2.cloned.1.call-done = bf16[512,14336]{1,0:T(8,128)(2,1)} async-done(((bf16[64,14336]{1,0:T(8,128)(2,1)}), bf16[512,14336]{1,0:T(8,128)(2,1)}) %all-gather.2.cloned.1.call-update) | async-done | bytes 14680080 | tf_op jit(solution)/shard_map/all_gather | solution.py:29
  302.2 20.0 %copy.19 = bf16[512,14336]{0,1:T(8,128)(2,1)} copy(bf16[512,14336]{1,0:T(8,128)(2,1)} %all-gather.2.cloned.1.call-done) | data formatting | bytes 29360128 | tf_op jit(solution)/shard_map/all_gather | solution.py:29
  322.2 19.9 %copy.21 = bf16[512,112,128]{2,0,1:T(8,128)(2,1)} copy(bf16[512,112,128]{0,2,1:T(8,128)(2,1)} %bitcast.11) | data formatting | bytes 29360128 | tf_op jit(solution)/shard_map/reshape | solution.py:36
  342.1 23.8 %gather_fusion = bf16[360,512,128]{2,1,0:T(8,128)(2,1)} fusion(bf16[512,112,128]{2,0,1:T(8,128)(2,1)} %copy.21, s32[1024]{0:T(1024)S(1)} %pad_clamp_fusion), kind=kCustom, calls=%fused_computation | custom fusion | bytes 94373280 | tf_op jit(solution)/shard_map/jit(_take)/gather | solution.py:37
  365.9 26.1 %fusion = f32[40,512,128,1]{1,2,3,0:T(8,128)} fusion(bf16[40,9,128,128]{3,2,1,0:T(8,128)(2,1)} %param.5, bf16[512,40,9,128]{3,0,2,1:T(8,128)(2,1)} %bitcast.12, pred[40,9]{1,0:T(8,128)(4,1)S(1)} %copy.18, bf16[40,9]{1,0:T(8,128)(2,1)S(1)} %compare_convert_fusion), kind=kOutput, calls=%fused_computation.1 | convolution fusion | flops 6086983680 | bytes 69469240 | tf_op jit(solution)/shard_map/srjb,rjcb->src/dot_general | solution.py:41
  392.0 11.4 %copy.22 = f32[512,5120]{1,0:T(8,128)} copy(f32[512,5120]{0,1:T(8,128)} %bitcast.13) | data formatting | bytes 20971520 | tf_op jit(solution)/shard_map/reshape | solution.py:43
  403.4 0.0 reduce-scatter.2.cloned.1.call-update
  403.4 209.8 %reduce-scatter.2.cloned.1.call-done = f32[64,5120]{1,0:T(8,128)} async-done(((f32[512,5120]{1,0:T(8,128)}), f32[64,5120]{1,0:T(8,128)}) %reduce-scatter.2.cloned.1.call-update) | async-done | bytes 1310736 | tf_op jit(solution)/shard_map/reduce_scatter | solution.py:42
  613.2 2.2 convert_element_type.11
  (3 shorter events, 0.0 us)
Async XLA Ops:
  6.5 295.7 %all-gather.2.cloned.1.call-start = ((), (), s32[]{:S(2)}) async-start(), calls=%async_computation.1 | async-start | bytes 16515072 | tf_op jit(solution)/shard_map/all_gather | solution.py:29
  7.9 10.6 %collective-permute-start = (bf16[64,4608]{1,0:T(8,128)(2,1)S(1)}, bf16[64,4608]{1,0:T(8,128)(2,1)S(1)}, u32[]{:S(2)}, u32[]{:S(2)}) collective-permute-start(bf16[64,4608]{1,0:T(8,128)(2,1)S(1)} %get-tuple-element.7), channel_id=1, source_target_pairs={{0,8},{8,16},{16,24},{24,32},{32,40},{40,48},{48,56},{56,64},{64,7... | collective-permute-start | bytes 1769480 | tf_op jit(solution)/shard_map/ppermute | solution.py:16
  11.7 13.3 %collective-permute-start.1 = (bf16[64,4608]{1,0:T(8,128)(2,1)S(1)}, bf16[64,4608]{1,0:T(8,128)(2,1)S(1)}, u32[]{:S(2)}, u32[]{:S(2)}) collective-permute-start(bf16[64,4608]{1,0:T(8,128)(2,1)S(1)} %get-tuple-element.8), channel_id=1, source_target_pairs={{8,0},{16,8},{24,16},{32,24},{40,32},{48,40},{56,48},{64,56},{72,6... | collective-permute-start | bytes 1769480 | tf_op jit(solution)/shard_map/ppermute | solution.py:17
  27.5 585.7 %reduce-scatter.2.cloned.1.call-start = ((), (), s32[]{:S(2)}) async-start(), calls=%async_computation.2 | async-start | bytes 11796480 | tf_op jit(solution)/shard_map/reduce_scatter | solution.py:42
Sparse Core Ops, SparseCore 0:
  27.6 274.5 all-gather.1
  403.6 209.6 reduce-scatter.1
where the time goes:
time: 625 us; the launch traced here: 622 us
  waiting for transfers between devices  494 us (79%)
  local copies, waits for them, and re-layouts  76.8 us (12%)
  matrix products  26.1 us (4%)
  between operations  13.5 us (2%)
    all_gather x1, waiting for transfers between devices, on_device(): gathered = lax.all_gather(banded, 'state', axis=0, tiled=True)  273 us
    reduce_scatter x1, waiting for transfers between devices, on_device(): lax.psum_scatter(result.reshape(row_count, shard_rows), 'state', scatter_...  210 us
    dot_general x1, matrix products, on_device(): jnp.einsum('srjb,rjcb->src', picked, blocks, preferred_element_type=jnp.f...  26.1 us
    gather x1, local copies, waits for them, and re-layouts, on_device(): jnp.take(state_part, relative, axis=1)  23.8 us
    all_gather x1, local copies, waits for them, and re-layouts, on_device(): gathered = lax.all_gather(banded, 'state', axis=0, tiled=True)  20 us
    reshape x1, local copies, waits for them, and re-layouts, on_device(): state_part = state_part.reshape(row_count, row_blocks + 2 * W, block_size)  19.9 us
  transfers between devices with their start and end apart: 4, of which 4 were waited for; matrix products, arithmetic and copies ran while one was open for 0% of the time, Pallas kernels for 0%

commit v1 on v0

v1 whole, which is shorter than its diff:
```python
import functools

import jax
import jax.numpy as jnp
from jax import lax
from jax.experimental import pallas as pl
from jax.experimental.pallas import tpu as pltpu
from jax.sharding import PartitionSpec as P

W = 36
X, Z_HI, Z_LO = 4, 2, 4
STEP_ROWS = 4


def x_perm(shift):
    return [(x * Z_HI + h, (x + shift) % X * Z_HI + h) for x in range(X) for h in range(Z_HI)]


def z_perm(shift, basis, state):
    inner = basis // Z_LO
    pairs = []
    for b in range(basis):
        z_lo, rest = divmod(b, inner)
        for s in range(state):
            x, z_hi = divmod(s, Z_HI)
            z = (z_hi * Z_LO + z_lo + shift) % (Z_HI * Z_LO)
            target = (z % Z_LO * inner + rest) * state + x * Z_HI + z // Z_LO
            pairs.append((b * state + s, target))
    return pairs


def from_x(value, shift):
    return lax.ppermute(value, "state", x_perm(-shift))


def across_z(value, step):
    pairs = z_perm(step, lax.axis_size("basis"), lax.axis_size("state"))
    return lax.ppermute(lax.ppermute(value, ("basis", "state"), pairs), ("basis", "state"), pairs)


def product_kernel(spans, slots, relative, live, blocks, *refs):
    pieces, outs, (panel, sems) = refs[:12], refs[12:16], refs[16:]
    states, size = outs[0].shape[0], blocks.shape[2]

    @pl.when(pl.program_id(0) == 0)
    def _():
        copies = []
        for i, piece in enumerate(pieces):
            source, width, target = spans[i % 3]
            copies.append(
                pltpu.make_async_copy(
                    piece.at[:, pl.ds(source, width)],
                    panel.at[pl.ds(i // 3 * states, states), pl.ds(target, width)],
                    sems.at[i],
                )
            )
        for copy in copies:
            copy.start()
        for copy in copies:
            copy.wait()

    for row in range(STEP_ROWS):
        base = (pl.program_id(0) * STEP_ROWS + row) * slots
        total = None
        for first in range(0, slots, 2):
            group = range(first, min(first + 2, slots))
            picked = [
                panel[:, pl.ds(pl.multiple_of(relative[base + k] * size, size), size)] for k in group
            ]
            weight = [
                jnp.where(live[base + k] > 0, blocks[row, k], jnp.zeros_like(blocks[row, k]))
                for k in group
            ]
            term = lax.dot_general(
                jnp.concatenate(picked, axis=1),
                jnp.concatenate(weight, axis=1),
                (((1,), (1,)), ((), ())),
                preferred_element_type=jnp.float32,
            )
            total = term if total is None else total + term
        for i, out in enumerate(outs):
            out[:, row * size : (row + 1) * size] = total[i * states : (i + 1) * states]


def product(half, relative, live, blocks, pieces):
    rows, slots, size, _ = blocks.shape
    part = rows // 2
    states = pieces[0].shape[0]
    lead = W - half * part if half else W
    tail = W if half else W - (rows - part)
    spans = (
        ((rows - lead) * size, lead * size, 0),
        (0, rows * size, lead * size),
        (0, tail * size, (lead + rows) * size),
    )
    steps = part // STEP_ROWS
    width = (part + 2 * W) * size
    grid_spec = pltpu.PrefetchScalarGridSpec(
        num_scalar_prefetch=2,
        grid=(steps,),
        in_specs=[
            pl.BlockSpec(
                (STEP_ROWS, slots, size, size), lambda i, *_: (half * steps + i, 0, 0, 0)
            )
        ]
        + [pl.BlockSpec(memory_space=pl.ANY)] * 12,
        out_specs=[pl.BlockSpec((states, STEP_ROWS * size), lambda i, *_: (0, i))] * 4,
        scratch_shapes=[
            pltpu.VMEM((4 * states, width), jnp.bfloat16),
            pltpu.SemaphoreType.DMA((12,)),
        ],
    )
    return pl.pallas_call(
        functools.partial(product_kernel, spans, slots),
        grid_spec=grid_spec,
        out_shape=[jax.ShapeDtypeStruct((states, part * size), jnp.float32)] * 4,
        compiler_params=pltpu.CompilerParams(vmem_limit_bytes=40 * 1024 * 1024),
        cost_estimate=pl.CostEstimate(
            flops=2 * part * slots * size * size * 4 * states * 3,
            bytes_accessed=4 * states * width * 2 + part * slots * size * size * 2,
            transcendentals=0,
        ),
    )(relative, live, blocks, *pieces)


def with_neighbours(piece):
    size = lax.axis_size("basis")
    up = [(i, i + 1) for i in range(size - 1)]
    down = [(j, i) for i, j in up]
    return (lax.ppermute(piece, "basis", up), piece, lax.ppermute(piece, "basis", down))


def on_device(vectors, blocks, columns, counts):
    rows, slots, size, _ = blocks.shape
    part = rows // 2
    first_block = lax.axis_index("basis") * rows - W
    relative = columns - first_block
    slot_index = lax.axis_index("state") * slots + jnp.arange(slots, dtype=jnp.int32)
    live = (slot_index[None, :] < counts[:, None]).astype(jnp.int32)

    cut = vectors.shape[0] // 2
    other = jnp.concatenate(
        [across_z(vectors[:cut], 2), across_z(vectors[cut:], -2)], axis=0
    )
    sums = []
    for mine, forward in ((other, -1), (vectors, 1)):
        right, left = from_x(mine, 1), from_x(mine, -1)
        opposite = from_x(right if forward == 1 else left, forward)
        pieces = [p for piece in (mine, right, left, opposite) for p in with_neighbours(piece)]
        partial = [
            product(
                h,
                (relative[h * part : (h + 1) * part] - h * part).reshape(-1),
                live[h * part : (h + 1) * part].reshape(-1),
                blocks,
                pieces,
            )
            for h in range(2)
        ]
        (own_a, right_a, left_a, far_a), (own_b, right_b, left_b, far_b) = partial
        total_a = own_a + from_x(right_a + from_x(far_a, -1), -1) + from_x(left_a, 1)
        total_b = own_b + from_x(right_b, -1) + from_x(left_b + from_x(far_b, 1), 1)
        sums.append((total_a, total_b))
    (away_a, away_b), (kept_a, kept_b) = sums
    sigma = jnp.concatenate(
        [kept_a + across_z(away_a, 2), kept_b + across_z(away_b, -2)], axis=1
    )
    return sigma.astype(jnp.bfloat16)


def solution(mesh):
    in_specs = (
        P("state", "basis"),
        P("basis", "state", None, None),
        P("basis", "state"),
        P("basis"),
    )
    out_specs = P("state", "basis")
    return jax.shard_map(
        on_device, mesh=mesh, in_specs=in_specs, out_specs=out_specs, check_vma=False
    )
```

time: 625 us -> 289 us (0.46)
  waiting for transfers between devices: 494 us -> 131 us
  starting transfers between devices: 5.73 us -> 107 us
  local copies, waits for them, and re-layouts: 76.8 us -> 9.25 us
  Pallas kernels: 0 us -> 36.5 us
  matrix products: 26.1 us -> 0 us
  between operations: 13.5 us -> 0.52 us
    all_gather x1 -> x0, waiting for transfers between devices: 273 us -> none  [on_device(): gathered = lax.all_gather(banded, 'state', axis=0, tiled=True)]
    reduce_scatter x1 -> x0, waiting for transfers between devices: 210 us -> none  [on_device(): lax.psum_scatter(result.reshape(row_count, shard_rows), 'state', scatter_...]
    ppermute x2 -> x42, waiting for transfers between devices: 11.4 us -> 131 us  [the longest x18 51.1 us: from_x(): return lax.ppermute(value, 'state', x_perm(-shift))]
    ppermute x2 -> x42, starting transfers between devices: 5.69 us -> 107 us  [the longest x8 39.6 us: with_neighbours(): lax.ppermute(piece, 'basis', up)]
    pallas_call x0 -> x4, Pallas kernels: none -> 36.5 us  [product(): pl.pallas_call(functools.partial(product_kernel, spans, slots), grid_spec...]
    reshape x3 -> x4, local copies, waits for them, and re-layouts: 31.5 us -> 0.37 us  [the longest x2 0.18 us: on_device(): (relative[h * part:(h + 1) * part] - h * part).reshape(-1)]
    dot_general x1 -> x0, matrix products: 26.1 us -> none  [on_device(): jnp.einsum('srjb,rjcb->src', picked, blocks, preferred_element_type=jnp.f...]
    gather x1 -> x0, local copies, waits for them, and re-layouts: 23.8 us -> none  [on_device(): jnp.take(state_part, relative, axis=1)]
  transfers between devices with their start and end apart: 4 -> 42, of which waited for: 4 -> 13; matrix products, arithmetic and copies ran while one was open for 0% -> 0% of each run, Pallas kernels for 0% -> 13%
where the time goes in v1:
time: 289 us; the launch traced here: 286 us
  waiting for transfers between devices  131 us (45%)
  starting transfers between devices  107 us (37%)
  Pallas kernels  36.5 us (13%)
  local copies, waits for them, and re-layouts  9.25 us (3%)
    ppermute x18, waiting for transfers between devices, from_x(): return lax.ppermute(value, 'state', x_perm(-shift))  51.1 us
    ppermute x4, waiting for transfers between devices, across_z(): lax.ppermute(lax.ppermute(value, ('basis', 'state'), pairs), ('basis', 's...  46 us
    ppermute x8, starting transfers between devices, with_neighbours(): lax.ppermute(piece, 'basis', up)  39.6 us
    pallas_call x4, Pallas kernels, product(): pl.pallas_call(functools.partial(product_kernel, spans, slots), grid_spec...  36.5 us
    ppermute x4, waiting for transfers between devices, across_z(): lax.ppermute(value, ('basis', 'state'), pairs)  31.6 us
    ppermute x18, starting transfers between devices, from_x(): return lax.ppermute(value, 'state', x_perm(-shift))  23.1 us
    ppermute x4, starting transfers between devices, across_z(): lax.ppermute(lax.ppermute(value, ('basis', 'state'), pairs), ('basis', 's...  18.6 us
    ppermute x8, starting transfers between devices, with_neighbours(): lax.ppermute(piece, 'basis', down)  15.5 us
  transfers between devices with their start and end apart: 42, of which 13 were waited for; matrix products, arithmetic and copies ran while one was open for 0% of the time, Pallas kernels for 13%

profile of v1, /device:TPU:25, one launch (start us, length us, event | category | flops | bytes accessed | tf_op | source)
XLA Modules:
  0.0 286.1 jit_solution(551588007455935565)
XLA Ops:
  1.2 3.1 %collective-permute-start.14 = (bf16[32,5120]{1,0:T(8,128)(2,1)S(1)}, bf16[32,5120]{1,0:T(8,128)(2,1)S(1)}, u32[]{:S(2)}, u32[]{:S(2)}) collective-permute-start(bf16[32,5120]{1,0:T(8,128)(2,1)S(1)} %get-tuple-element.38), channel_id=1, source_target_pairs={{0,128},{1,129},{2,130},{3,131},{4,132},{5,133},{6,134},{7,135},{8... | collective-permute-start | bytes 983048 | tf_op jit(solution)/shard_map/ppermute | solution.py:38
  4.3 3.1 %collective-permute-start.16 = (bf16[32,5120]{1,0:T(8,128)(2,1)S(1)}, bf16[32,5120]{1,0:T(8,128)(2,1)S(1)}, u32[]{:S(2)}, u32[]{:S(2)}) collective-permute-start(bf16[32,5120]{1,0:T(8,128)(2,1)S(1)} %get-tuple-element.37), channel_id=1, source_target_pairs={{0,129},{1,128},{2,131},{3,130},{4,133},{5,132},{6,135},{7,134},{8... | collective-permute-start | bytes 983048 | tf_op jit(solution)/shard_map/ppermute | solution.py:38
  7.4 9.4 %collective-permute-done.14 = bf16[32,5120]{1,0:T(8,128)(2,1)S(1)} collective-permute-done((bf16[32,5120]{1,0:T(8,128)(2,1)S(1)}, bf16[32,5120]{1,0:T(8,128)(2,1)S(1)}, u32[]{:S(2)}, u32[]{:S(2)}) %collective-permute-start.14) | collective-permute-done | bytes 327712 | tf_op jit(solution)/shard_map/ppermute | solution.py:38
  16.7 5.6 %collective-permute-start.15 = (bf16[32,5120]{1,0:T(8,128)(2,1)S(1)}, bf16[32,5120]{1,0:T(8,128)(2,1)S(1)}, u32[]{:S(2)}, u32[]{:S(2)}) collective-permute-start(bf16[32,5120]{1,0:T(8,128)(2,1)S(1)} %collective-permute-done.14), channel_id=1, source_target_pairs={{0,128},{1,129},{2,130},{3,131},{4,132},{5,133},{6,134},{7,135},{8... | collective-permute-start | bytes 983048 | tf_op jit(solution)/shard_map/ppermute | solution.py:38
  22.4 2.5 collective-permute-start.2
  24.8 3.2 %collective-permute-start = (bf16[64,5120]{1,0:T(8,128)(2,1)S(1)}, bf16[64,5120]{1,0:T(8,128)(2,1)S(1)}, u32[]{:S(2)}, u32[]{:S(2)}) collective-permute-start(bf16[64,5120]{1,0:T(8,128)(2,1)S(1)} %copy-done), channel_id=1, source_target_pairs={{0,8},{8,16},{16,24},{24,32},{32,40},{40,48},{48,56},{56,64},{64,7... | collective-permute-start | bytes 1966088 | tf_op jit(solution)/shard_map/ppermute | solution.py:130
  28.1 2.1 collective-permute-start.1
  31.6 9.4 %collective-permute-start.17 = (bf16[32,5120]{1,0:T(8,128)(2,1)S(1)}, bf16[32,5120]{1,0:T(8,128)(2,1)S(1)}, u32[]{:S(2)}, u32[]{:S(2)}) collective-permute-start(bf16[32,5120]{1,0:T(8,128)(2,1)S(1)} %collective-permute-done.16), channel_id=1, source_target_pairs={{0,129},{1,128},{2,131},{3,130},{4,133},{5,132},{6,135},{7,134},{8... | collective-permute-start | bytes 983048 | tf_op jit(solution)/shard_map/ppermute | solution.py:38
  41.0 13.3 %collective-permute-done.17 = bf16[32,5120]{1,0:T(8,128)(2,1)S(1)} collective-permute-done((bf16[32,5120]{1,0:T(8,128)(2,1)S(1)}, bf16[32,5120]{1,0:T(8,128)(2,1)S(1)}, u32[]{:S(2)}, u32[]{:S(2)}) %collective-permute-start.17) | collective-permute-done | bytes 327712 | tf_op jit(solution)/shard_map/ppermute | solution.py:38
  57.2 7.9 %collective-permute-start.18 = (bf16[64,5120]{1,0:T(8,128)(2,1)S(1)}, bf16[64,5120]{1,0:T(8,128)(2,1)S(1)}, u32[]{:S(2)}, u32[]{:S(2)}) collective-permute-start(bf16[64,5120]{1,0:T(8,128)(2,1)S(1)} %constant_dynamic-update-slice_fusion.refs_1_), channel_id=1, source_target_pairs={{0,8},{8,16},{16,24},{24,32},{32,40},{40,48},{48,56},{56,64},{64,7... | collective-permute-start | bytes 1966088 | tf_op jit(solution)/shard_map/ppermute | solution.py:130
  69.6 1.9 collective-permute-done.23.refs_7_
  71.5 4.1 %collective-permute-start.3 = (bf16[64,5120]{1,0:T(8,128)(2,1)S(1)}, bf16[64,5120]{1,0:T(8,128)(2,1)S(1)}, u32[]{:S(2)}, u32[]{:S(2)}) collective-permute-start(bf16[64,5120]{1,0:T(8,128)(2,1)S(1)} %collective-permute-done.2.refs_4_), channel_id=1, source_target_pairs={{0,8},{8,16},{16,24},{24,32},{32,40},{40,48},{48,56},{56,64},{64,7... | collective-permute-start | bytes 1966088 | tf_op jit(solution)/shard_map/ppermute | solution.py:130
  76.6 4.5 %collective-permute-start.24 = (bf16[64,5120]{1,0:T(8,128)(2,1)}, bf16[64,5120]{1,0:T(8,128)(2,1)S(1)}, u32[]{:S(2)}, u32[]{:S(2)}) collective-permute-start(bf16[64,5120]{1,0:T(8,128)(2,1)} %collective-permute-done.23.refs_7_), channel_id=1, source_target_pairs={{0,8},{8,16},{16,24},{24,32},{32,40},{40,48},{48,56},{56,64},{64,7... | collective-permute-start | bytes 1966088 | tf_op jit(solution)/shard_map/ppermute | solution.py:130
  85.2 4.3 %collective-permute-start.21 = (bf16[64,5120]{1,0:T(8,128)(2,1)}, bf16[64,5120]{1,0:T(8,128)(2,1)}, u32[]{:S(2)}, u32[]{:S(2)}) collective-permute-start(bf16[64,5120]{1,0:T(8,128)(2,1)} %collective-permute-done.20.refs_4_), channel_id=1, source_target_pairs={{0,8},{8,16},{16,24},{24,32},{32,40},{40,48},{48,56},{56,64},{64,7... | collective-permute-start | bytes 1966088 | tf_op jit(solution)/shard_map/ppermute | solution.py:130
  93.4 4.7 %collective-permute-start.27 = (bf16[64,5120]{1,0:T(8,128)(2,1)}, bf16[64,5120]{1,0:T(8,128)(2,1)}, u32[]{:S(2)}, u32[]{:S(2)}) collective-permute-start(bf16[64,5120]{1,0:T(8,128)(2,1)} %collective-permute-done.26.refs_10_), channel_id=1, source_target_pairs={{0,8},{8,16},{16,24},{24,32},{32,40},{40,48},{48,56},{56,64},{64,7... | collective-permute-start | bytes 1966088 | tf_op jit(solution)/shard_map/ppermute | solution.py:130
  103.0 5.8 %collective-permute-start.6 = (bf16[64,5120]{1,0:T(8,128)(2,1)S(1)}, bf16[64,5120]{1,0:T(8,128)(2,1)}, u32[]{:S(2)}, u32[]{:S(2)}) collective-permute-start(bf16[64,5120]{1,0:T(8,128)(2,1)S(1)} %collective-permute-done.5.refs_7_), channel_id=1, source_target_pairs={{0,8},{8,16},{16,24},{24,32},{32,40},{40,48},{48,56},{56,64},{64,7... | collective-permute-start | bytes 1966088 | tf_op jit(solution)/shard_map/ppermute | solution.py:130
  113.3 5.1 %collective-permute-start.9 = (bf16[64,5120]{1,0:T(8,128)(2,1)}, bf16[64,5120]{1,0:T(8,128)(2,1)}, u32[]{:S(2)}, u32[]{:S(2)}) collective-permute-start(bf16[64,5120]{1,0:T(8,128)(2,1)} %copy-done.3), channel_id=1, source_target_pairs={{0,8},{8,16},{16,24},{24,32},{32,40},{40,48},{48,56},{56,64},{64,7... | collective-permute-start | bytes 1966088 | tf_op jit(solution)/shard_map/ppermute | solution.py:130
  122.3 9.3 %shard_map.47 = (f32[64,2560]{1,0:T(8,128)S(1)}, f32[64,2560]{1,0:T(8,128)S(1)}, f32[64,2560]{1,0:T(8,128)S(1)}, f32[64,2560]{1,0:T(8,128)S(1)}) custom-call(s32[180]{0:T(256)S(1)} %reshape.21.relative, s32[180]{0:T(256)S(1)} %reshape.22.live, bf16[40,9,128,128]{3,2,1,0:T(8,128)(2,1)} %blocks.7, bf16[64,5120]{1,0:T(8,128)(2,1)S(1)} %copy-done.8, ...), custom_call_target="tpu_custom_call" | custom-call | flops 4529848320 | bytes 11927552 | tf_op jit(solution)/shard_map/pallas_call | solution.py:113
  134.4 8.8 %shard_map.46 = (f32[64,2560]{1,0:T(8,128)S(1)}, f32[64,2560]{1,0:T(8,128)S(1)}, f32[64,2560]{1,0:T(8,128)S(1)}, f32[64,2560]{1,0:T(8,128)S(1)}) custom-call(s32[180]{0:T(256)S(1)} %reshape.21.relative, s32[180]{0:T(256)S(1)} %reshape.22.live, bf16[40,9,128,128]{3,2,1,0:T(8,128)(2,1)} %blocks.7, bf16[64,5120]{1,0:T(8,128)(2,1)S(1)} %collective-permute-done.refs_0_, ...), custom_call_target="tpu_custom_call" | custom-call | flops 4529848320 | bytes 11927552 | tf_op jit(solution)/shard_map/pallas_call | solution.py:113
  143.8 9.4 %shard_map.49 = (f32[64,2560]{1,0:T(8,128)S(1)}, f32[64,2560]{1,0:T(8,128)S(1)}, f32[64,2560]{1,0:T(8,128)S(1)}, f32[64,2560]{1,0:T(8,128)S(1)}) custom-call(s32[180]{0:T(256)S(1)} %reshape.23.relative, s32[180]{0:T(256)S(1)} %reshape.24.live, bf16[40,9,128,128]{3,2,1,0:T(8,128)(2,1)} %blocks.7, bf16[64,5120]{1,0:T(8,128)(2,1)S(1)} %copy-done.8, ...), custom_call_target="tpu_custom_call" | custom-call | flops 4529848320 | bytes 11927552 | tf_op jit(solution)/shard_map/pallas_call | solution.py:113
  153.2 2.3 collective-permute-start.38
  157.1 2.0 collective-permute-start.13
  159.1 8.9 %shard_map.48 = (f32[64,2560]{1,0:T(8,128)S(1)}, f32[64,2560]{1,0:T(8,128)S(1)}, f32[64,2560]{1,0:T(8,128)S(1)}, f32[64,2560]{1,0:T(8,128)S(1)}) custom-call(s32[180]{0:T(256)S(1)} %reshape.23.relative, s32[180]{0:T(256)S(1)} %reshape.24.live, bf16[40,9,128,128]{3,2,1,0:T(8,128)(2,1)} %blocks.7, bf16[64,5120]{1,0:T(8,128)(2,1)S(1)} %collective-permute-done.refs_0_, ...), custom_call_target="tpu_custom_call" | custom-call | flops 4529848320 | bytes 11927552 | tf_op jit(solution)/shard_map/pallas_call | solution.py:113
  168.2 1.9 collective-permute-done.38
  171.1 13.0 %collective-permute-done.31 = f32[64,2560]{1,0:T(8,128)S(1)} collective-permute-done((f32[64,2560]{1,0:T(8,128)S(1)}, f32[64,2560]{1,0:T(8,128)S(1)}, u32[]{:S(2)}, u32[]{:S(2)}) %collective-permute-start.31) | collective-permute-done | bytes 655392 | tf_op jit(solution)/shard_map/ppermute | solution.py:33
  184.2 3.4 %collective-permute-start.39 = (f32[64,2560]{1,0:T(8,128)S(1)}, f32[64,2560]{1,0:T(8,128)S(1)}, u32[]{:S(2)}, u32[]{:S(2)}) collective-permute-start(f32[64,2560]{1,0:T(8,128)S(1)} %add.67), channel_id=1, source_target_pairs={{0,6},{1,7},{2,0},{3,1},{4,2},{5,3},{6,4},{7,5},{8,14},{9,15},{10,... | collective-permute-start | bytes 1966088 | tf_op jit(solution)/shard_map/ppermute | solution.py:33
  187.7 3.5 %collective-permute-start.32 = (f32[64,2560]{1,0:T(8,128)S(1)}, f32[64,2560]{1,0:T(8,128)S(1)}, u32[]{:S(2)}, u32[]{:S(2)}) collective-permute-start(f32[64,2560]{1,0:T(8,128)S(1)} %add_add_fusion.1), channel_id=1, source_target_pairs={{0,128},{1,129},{2,130},{3,131},{4,132},{5,133},{6,134},{7,135},{8... | collective-permute-start | bytes 1966088 | tf_op jit(solution)/shard_map/ppermute | solution.py:38
  191.2 31.7 %collective-permute-done.39 = f32[64,2560]{1,0:T(8,128)S(1)} collective-permute-done((f32[64,2560]{1,0:T(8,128)S(1)}, f32[64,2560]{1,0:T(8,128)S(1)}, u32[]{:S(2)}, u32[]{:S(2)}) %collective-permute-start.39) | collective-permute-done | bytes 655392 | tf_op jit(solution)/shard_map/ppermute | solution.py:33
  224.6 3.0 %collective-permute-start.33 = (f32[64,2560]{1,0:T(8,128)S(1)}, f32[64,2560]{1,0:T(8,128)S(1)}, u32[]{:S(2)}, u32[]{:S(2)}) collective-permute-start(f32[64,2560]{1,0:T(8,128)S(1)} %collective-permute-done.32), channel_id=1, source_target_pairs={{0,128},{1,129},{2,130},{3,131},{4,132},{5,133},{6,134},{7,135},{8... | collective-permute-start | bytes 1966088 | tf_op jit(solution)/shard_map/ppermute | solution.py:38
  228.7 2.0 collective-permute-start.36
  230.7 22.3 %collective-permute-done.40 = f32[64,2560]{1,0:T(8,128)S(1)} collective-permute-done((f32[64,2560]{1,0:T(8,128)S(1)}, f32[64,2560]{1,0:T(8,128)S(1)}, u32[]{:S(2)}, u32[]{:S(2)}) %collective-permute-start.40) | collective-permute-done | bytes 655392 | tf_op jit(solution)/shard_map/ppermute | solution.py:38
  253.7 31.3 %collective-permute-done.41 = f32[64,2560]{1,0:T(8,128)S(1)} collective-permute-done((f32[64,2560]{1,0:T(8,128)S(1)}, f32[64,2560]{1,0:T(8,128)S(1)}, u32[]{:S(2)}, u32[]{:S(2)}) %collective-permute-start.41) | collective-permute-done | bytes 655392 | tf_op jit(solution)/shard_map/ppermute | solution.py:38
  (113 shorter events, 42.7 us)
Async XLA Ops:
  4.3 23.8 %collective-permute-start.16 = (bf16[32,5120]{1,0:T(8,128)(2,1)S(1)}, bf16[32,5120]{1,0:T(8,128)(2,1)S(1)}, u32[]{:S(2)}, u32[]{:S(2)}) collective-permute-start(bf16[32,5120]{1,0:T(8,128)(2,1)S(1)} %get-tuple-element.37), channel_id=1, source_target_pairs={{0,129},{1,128},{2,131},{3,130},{4,133},{5,132},{6,135},{7,134},{8... | collective-permute-start | bytes 983048 | tf_op jit(solution)/shard_map/ppermute | solution.py:38
  22.4 33.3 %collective-permute-start.2 = (bf16[64,5120]{1,0:T(8,128)(2,1)S(1)}, bf16[64,5120]{1,0:T(8,128)(2,1)S(1)}, u32[]{:S(2)}, u32[]{:S(2)}) collective-permute-start(bf16[64,5120]{1,0:T(8,128)(2,1)S(1)} %copy-done), channel_id=1, source_target_pairs={{0,6},{1,7},{2,0},{3,1},{4,2},{5,3},{6,4},{7,5},{8,14},{9,15},{10,... | collective-permute-start | bytes 1966088 | tf_op jit(solution)/shard_map/ppermute | solution.py:33
  24.8 32.4 %collective-permute-start.5 = (bf16[64,5120]{1,0:T(8,128)(2,1)S(1)}, bf16[64,5120]{1,0:T(8,128)(2,1)S(1)}, u32[]{:S(2)}, u32[]{:S(2)}) collective-permute-start(bf16[64,5120]{1,0:T(8,128)(2,1)S(1)} %copy-done), channel_id=1, source_target_pairs={{0,2},{1,3},{2,4},{3,5},{4,6},{5,7},{6,0},{7,1},{8,10},{9,11},{10,... | collective-permute-start | bytes 1966088 | tf_op jit(solution)/shard_map/ppermute | solution.py:33
  24.8 40.3 %collective-permute-start = (bf16[64,5120]{1,0:T(8,128)(2,1)S(1)}, bf16[64,5120]{1,0:T(8,128)(2,1)S(1)}, u32[]{:S(2)}, u32[]{:S(2)}) collective-permute-start(bf16[64,5120]{1,0:T(8,128)(2,1)S(1)} %copy-done), channel_id=1, source_target_pairs={{0,8},{8,16},{16,24},{24,32},{32,40},{40,48},{48,56},{56,64},{64,7... | collective-permute-start | bytes 1966088 | tf_op jit(solution)/shard_map/ppermute | solution.py:130
  28.1 39.0 %collective-permute-start.1 = (bf16[64,5120]{1,0:T(8,128)(2,1)S(1)}, bf16[64,5120]{1,0:T(8,128)(2,1)S(1)}, u32[]{:S(2)}, u32[]{:S(2)}) collective-permute-start(bf16[64,5120]{1,0:T(8,128)(2,1)S(1)} %copy-done), channel_id=1, source_target_pairs={{8,0},{16,8},{24,16},{32,24},{40,32},{48,40},{56,48},{64,56},{72,6... | collective-permute-start | bytes 1966088 | tf_op jit(solution)/shard_map/ppermute | solution.py:130
  31.6 22.7 %collective-permute-start.17 = (bf16[32,5120]{1,0:T(8,128)(2,1)S(1)}, bf16[32,5120]{1,0:T(8,128)(2,1)S(1)}, u32[]{:S(2)}, u32[]{:S(2)}) collective-permute-start(bf16[32,5120]{1,0:T(8,128)(2,1)S(1)} %collective-permute-done.16), channel_id=1, source_target_pairs={{0,129},{1,128},{2,131},{3,130},{4,133},{5,132},{6,135},{7,134},{8... | collective-permute-start | bytes 983048 | tf_op jit(solution)/shard_map/ppermute | solution.py:38
  55.6 20.0 %collective-permute-start.20 = (bf16[64,5120]{1,0:T(8,128)(2,1)S(1)}, bf16[64,5120]{1,0:T(8,128)(2,1)}, u32[]{:S(2)}, u32[]{:S(2)}) collective-permute-start(bf16[64,5120]{1,0:T(8,128)(2,1)S(1)} %constant_dynamic-update-slice_fusion.refs_1_), channel_id=1, source_target_pairs={{0,6},{1,7},{2,0},{3,1},{4,2},{5,3},{6,4},{7,5},{8,14},{9,15},{10,... | collective-permute-start | bytes 1966088 | tf_op jit(solution)/shard_map/ppermute | solution.py:33
  57.2 18.5 %collective-permute-start.18 = (bf16[64,5120]{1,0:T(8,128)(2,1)S(1)}, bf16[64,5120]{1,0:T(8,128)(2,1)S(1)}, u32[]{:S(2)}, u32[]{:S(2)}) collective-permute-start(bf16[64,5120]{1,0:T(8,128)(2,1)S(1)} %constant_dynamic-update-slice_fusion.refs_1_), channel_id=1, source_target_pairs={{0,8},{8,16},{16,24},{24,32},{32,40},{40,48},{48,56},{56,64},{64,7... | collective-permute-start | bytes 1966088 | tf_op jit(solution)/shard_map/ppermute | solution.py:130
  71.5 18.1 %collective-permute-start.3 = (bf16[64,5120]{1,0:T(8,128)(2,1)S(1)}, bf16[64,5120]{1,0:T(8,128)(2,1)S(1)}, u32[]{:S(2)}, u32[]{:S(2)}) collective-permute-start(bf16[64,5120]{1,0:T(8,128)(2,1)S(1)} %collective-permute-done.2.refs_4_), channel_id=1, source_target_pairs={{0,8},{8,16},{16,24},{24,32},{32,40},{40,48},{48,56},{56,64},{64,7... | collective-permute-start | bytes 1966088 | tf_op jit(solution)/shard_map/ppermute | solution.py:130
  76.6 21.6 %collective-permute-start.24 = (bf16[64,5120]{1,0:T(8,128)(2,1)}, bf16[64,5120]{1,0:T(8,128)(2,1)S(1)}, u32[]{:S(2)}, u32[]{:S(2)}) collective-permute-start(bf16[64,5120]{1,0:T(8,128)(2,1)} %collective-permute-done.23.refs_7_), channel_id=1, source_target_pairs={{0,8},{8,16},{16,24},{24,32},{32,40},{40,48},{48,56},{56,64},{64,7... | collective-permute-start | bytes 1966088 | tf_op jit(solution)/shard_map/ppermute | solution.py:130
  81.9 19.1 %collective-permute-start.25 = (bf16[64,5120]{1,0:T(8,128)(2,1)}, bf16[64,5120]{1,0:T(8,128)(2,1)}, u32[]{:S(2)}, u32[]{:S(2)}) collective-permute-start(bf16[64,5120]{1,0:T(8,128)(2,1)} %collective-permute-done.23.refs_7_), channel_id=1, source_target_pairs={{8,0},{16,8},{24,16},{32,24},{40,32},{48,40},{56,48},{64,56},{72,6... | collective-permute-start | bytes 1966088 | tf_op jit(solution)/shard_map/ppermute | solution.py:130
  90.4 18.3 %collective-permute-start.22 = (bf16[64,5120]{1,0:T(8,128)(2,1)}, bf16[64,5120]{1,0:T(8,128)(2,1)}, u32[]{:S(2)}, u32[]{:S(2)}) collective-permute-start(bf16[64,5120]{1,0:T(8,128)(2,1)} %collective-permute-done.20.refs_4_), channel_id=1, source_target_pairs={{8,0},{16,8},{24,16},{32,24},{40,32},{48,40},{56,48},{64,56},{72,6... | collective-permute-start | bytes 1966088 | tf_op jit(solution)/shard_map/ppermute | solution.py:130
  101.0 30.6 %collective-permute-start.4 = (bf16[64,5120]{1,0:T(8,128)(2,1)S(1)}, bf16[64,5120]{1,0:T(8,128)(2,1)}, u32[]{:S(2)}, u32[]{:S(2)}) collective-permute-start(bf16[64,5120]{1,0:T(8,128)(2,1)S(1)} %collective-permute-done.2.refs_4_), channel_id=1, source_target_pairs={{8,0},{16,8},{24,16},{32,24},{40,32},{48,40},{56,48},{64,56},{72,6... | collective-permute-start | bytes 1966088 | tf_op jit(solution)/shard_map/ppermute | solution.py:130
  103.0 29.5 %collective-permute-start.6 = (bf16[64,5120]{1,0:T(8,128)(2,1)S(1)}, bf16[64,5120]{1,0:T(8,128)(2,1)}, u32[]{:S(2)}, u32[]{:S(2)}) collective-permute-start(bf16[64,5120]{1,0:T(8,128)(2,1)S(1)} %collective-permute-done.5.refs_7_), channel_id=1, source_target_pairs={{0,8},{8,16},{16,24},{24,32},{32,40},{40,48},{48,56},{56,64},{64,7... | collective-permute-start | bytes 1966088 | tf_op jit(solution)/shard_map/ppermute | solution.py:130
  108.7 23.7 %collective-permute-start.7 = (bf16[64,5120]{1,0:T(8,128)(2,1)S(1)}, bf16[64,5120]{1,0:T(8,128)(2,1)}, u32[]{:S(2)}, u32[]{:S(2)}) collective-permute-start(bf16[64,5120]{1,0:T(8,128)(2,1)S(1)} %collective-permute-done.5.refs_7_), channel_id=1, source_target_pairs={{8,0},{16,8},{24,16},{32,24},{40,32},{48,40},{56,48},{64,56},{72,6... | collective-permute-start | bytes 1966088 | tf_op jit(solution)/shard_map/ppermute | solution.py:130
  110.7 23.7 %collective-permute-start.10 = (bf16[64,5120]{1,0:T(8,128)(2,1)}, bf16[64,5120]{1,0:T(8,128)(2,1)}, u32[]{:S(2)}, u32[]{:S(2)}) collective-permute-start(bf16[64,5120]{1,0:T(8,128)(2,1)} %copy-done.3), channel_id=1, source_target_pairs={{8,0},{16,8},{24,16},{32,24},{40,32},{48,40},{56,48},{64,56},{72,6... | collective-permute-start | bytes 1966088 | tf_op jit(solution)/shard_map/ppermute | solution.py:130
  113.3 21.1 %collective-permute-start.9 = (bf16[64,5120]{1,0:T(8,128)(2,1)}, bf16[64,5120]{1,0:T(8,128)(2,1)}, u32[]{:S(2)}, u32[]{:S(2)}) collective-permute-start(bf16[64,5120]{1,0:T(8,128)(2,1)} %copy-done.3), channel_id=1, source_target_pairs={{0,8},{8,16},{16,24},{24,32},{32,40},{40,48},{48,56},{56,64},{64,7... | collective-permute-start | bytes 1966088 | tf_op jit(solution)/shard_map/ppermute | solution.py:130
  131.7 24.6 %collective-permute-start.29 = (f32[64,2560]{1,0:T(8,128)S(1)}, f32[64,2560]{1,0:T(8,128)S(1)}, u32[]{:S(2)}, u32[]{:S(2)}) collective-permute-start(f32[64,2560]{1,0:T(8,128)S(1)} %get-tuple-element.27), channel_id=1, source_target_pairs={{0,2},{1,3},{2,4},{3,5},{4,6},{5,7},{6,0},{7,1},{8,10},{9,11},{10,... | collective-permute-start | bytes 1966088 | tf_op jit(solution)/shard_map/ppermute | solution.py:33
  143.2 24.8 %collective-permute-start.11 = (f32[64,2560]{1,0:T(8,128)S(1)}, f32[64,2560]{1,0:T(8,128)S(1)}, u32[]{:S(2)}, u32[]{:S(2)}) collective-permute-start(f32[64,2560]{1,0:T(8,128)S(1)} %get-tuple-element.23), channel_id=1, source_target_pairs={{0,2},{1,3},{2,4},{3,5},{4,6},{5,7},{6,0},{7,1},{8,10},{9,11},{10,... | collective-permute-start | bytes 1966088 | tf_op jit(solution)/shard_map/ppermute | solution.py:33
  155.5 28.7 %collective-permute-start.31 = (f32[64,2560]{1,0:T(8,128)S(1)}, f32[64,2560]{1,0:T(8,128)S(1)}, u32[]{:S(2)}, u32[]{:S(2)}) collective-permute-start(f32[64,2560]{1,0:T(8,128)S(1)} %get-tuple-element.28), channel_id=1, source_target_pairs={{0,6},{1,7},{2,0},{3,1},{4,2},{5,3},{6,4},{7,5},{8,14},{9,15},{10,... | collective-permute-start | bytes 1966088 | tf_op jit(solution)/shard_map/ppermute | solution.py:33
  156.4 31.2 %collective-permute-start.30 = (f32[64,2560]{1,0:T(8,128)S(1)}, f32[64,2560]{1,0:T(8,128)S(1)}, u32[]{:S(2)}, u32[]{:S(2)}) collective-permute-start(f32[64,2560]{1,0:T(8,128)S(1)} %add.59), channel_id=1, source_target_pairs={{0,2},{1,3},{2,4},{3,5},{4,6},{5,7},{6,0},{7,1},{8,10},{9,11},{10,... | collective-permute-start | bytes 1966088 | tf_op jit(solution)/shard_map/ppermute | solution.py:33
  157.1 71.6 %collective-permute-start.13 = (f32[64,2560]{1,0:T(8,128)S(1)}, f32[64,2560]{1,0:T(8,128)S(1)}, u32[]{:S(2)}, u32[]{:S(2)}) collective-permute-start(f32[64,2560]{1,0:T(8,128)S(1)} %get-tuple-element.24), channel_id=1, source_target_pairs={{0,6},{1,7},{2,0},{3,1},{4,2},{5,3},{6,4},{7,5},{8,14},{9,15},{10,... | collective-permute-start | bytes 1966088 | tf_op jit(solution)/shard_map/ppermute | solution.py:33
  168.0 59.6 %collective-permute-start.35 = (f32[64,2560]{1,0:T(8,128)S(1)}, f32[64,2560]{1,0:T(8,128)S(1)}, u32[]{:S(2)}, u32[]{:S(2)}) collective-permute-start(f32[64,2560]{1,0:T(8,128)S(1)} %get-tuple-element.32), channel_id=1, source_target_pairs={{0,6},{1,7},{2,0},{3,1},{4,2},{5,3},{6,4},{7,5},{8,14},{9,15},{10,... | collective-permute-start | bytes 1966088 | tf_op jit(solution)/shard_map/ppermute | solution.py:33
  170.1 21.0 %collective-permute-start.37 = (f32[64,2560]{1,0:T(8,128)S(1)}, f32[64,2560]{1,0:T(8,128)S(1)}, u32[]{:S(2)}, u32[]{:S(2)}) collective-permute-start(f32[64,2560]{1,0:T(8,128)S(1)} %get-tuple-element.34), channel_id=1, source_target_pairs={{0,2},{1,3},{2,4},{3,5},{4,6},{5,7},{6,0},{7,1},{8,10},{9,11},{10,... | collective-permute-start | bytes 1966088 | tf_op jit(solution)/shard_map/ppermute | solution.py:33
  184.2 38.7 %collective-permute-start.39 = (f32[64,2560]{1,0:T(8,128)S(1)}, f32[64,2560]{1,0:T(8,128)S(1)}, u32[]{:S(2)}, u32[]{:S(2)}) collective-permute-start(f32[64,2560]{1,0:T(8,128)S(1)} %add.67), channel_id=1, source_target_pairs={{0,6},{1,7},{2,0},{3,1},{4,2},{5,3},{6,4},{7,5},{8,14},{9,15},{10,... | collective-permute-start | bytes 1966088 | tf_op jit(solution)/shard_map/ppermute | solution.py:33
  187.7 36.9 %collective-permute-start.32 = (f32[64,2560]{1,0:T(8,128)S(1)}, f32[64,2560]{1,0:T(8,128)S(1)}, u32[]{:S(2)}, u32[]{:S(2)}) collective-permute-start(f32[64,2560]{1,0:T(8,128)S(1)} %add_add_fusion.1), channel_id=1, source_target_pairs={{0,128},{1,129},{2,130},{3,131},{4,132},{5,133},{6,134},{7,135},{8... | collective-permute-start | bytes 1966088 | tf_op jit(solution)/shard_map/ppermute | solution.py:38
  223.0 30.0 %collective-permute-start.40 = (f32[64,2560]{1,0:T(8,128)S(1)}, f32[64,2560]{1,0:T(8,128)S(1)}, u32[]{:S(2)}, u32[]{:S(2)}) collective-permute-start(f32[64,2560]{1,0:T(8,128)S(1)} %add_add_fusion), channel_id=1, source_target_pairs={{0,129},{1,128},{2,131},{3,130},{4,133},{5,132},{6,135},{7,134},{8... | collective-permute-start | bytes 1966088 | tf_op jit(solution)/shard_map/ppermute | solution.py:38
  223.1 30.5 %collective-permute-start.12 = (f32[64,2560]{1,0:T(8,128)S(1)}, f32[64,2560]{1,0:T(8,128)S(1)}, u32[]{:S(2)}, u32[]{:S(2)}) collective-permute-start(f32[64,2560]{1,0:T(8,128)S(1)} %add.56), channel_id=1, source_target_pairs={{0,2},{1,3},{2,4},{3,5},{4,6},{5,7},{6,0},{7,1},{8,10},{9,11},{10,... | collective-permute-start | bytes 1966088 | tf_op jit(solution)/shard_map/ppermute | solution.py:33
  224.6 29.0 %collective-permute-start.33 = (f32[64,2560]{1,0:T(8,128)S(1)}, f32[64,2560]{1,0:T(8,128)S(1)}, u32[]{:S(2)}, u32[]{:S(2)}) collective-permute-start(f32[64,2560]{1,0:T(8,128)S(1)} %collective-permute-done.32), channel_id=1, source_target_pairs={{0,128},{1,129},{2,130},{3,131},{4,132},{5,133},{6,134},{7,135},{8... | collective-permute-start | bytes 1966088 | tf_op jit(solution)/shard_map/ppermute | solution.py:38
  227.6 26.1 %collective-permute-start.34 = (f32[64,2560]{1,0:T(8,128)S(1)}, f32[64,2560]{1,0:T(8,128)S(1)}, u32[]{:S(2)}, u32[]{:S(2)}) collective-permute-start(f32[64,2560]{1,0:T(8,128)S(1)} %get-tuple-element.30), channel_id=1, source_target_pairs={{0,2},{1,3},{2,4},{3,5},{4,6},{5,7},{6,0},{7,1},{8,10},{9,11},{10,... | collective-permute-start | bytes 1966088 | tf_op jit(solution)/shard_map/ppermute | solution.py:33
  228.7 25.0 %collective-permute-start.36 = (f32[64,2560]{1,0:T(8,128)S(1)}, f32[64,2560]{1,0:T(8,128)S(1)}, u32[]{:S(2)}, u32[]{:S(2)}) collective-permute-start(f32[64,2560]{1,0:T(8,128)S(1)} %add.64), channel_id=1, source_target_pairs={{0,6},{1,7},{2,0},{3,1},{4,2},{5,3},{6,4},{7,5},{8,14},{9,15},{10,... | collective-permute-start | bytes 1966088 | tf_op jit(solution)/shard_map/ppermute | solution.py:33
  253.0 32.0 %collective-permute-start.41 = (f32[64,2560]{1,0:T(8,128)S(1)}, f32[64,2560]{1,0:T(8,128)S(1)}, u32[]{:S(2)}, u32[]{:S(2)}) collective-permute-start(f32[64,2560]{1,0:T(8,128)S(1)} %collective-permute-done.40), channel_id=1, source_target_pairs={{0,129},{1,128},{2,131},{3,130},{4,133},{5,132},{6,135},{7,134},{8... | collective-permute-start | bytes 1966088 | tf_op jit(solution)/shard_map/ppermute | solution.py:38
  (27 other events, 478.7 us)

commit v2 on v0

v2 whole, which is shorter than its diff:
```python
import functools

import jax
import jax.numpy as jnp
from jax import lax
from jax.experimental import pallas as pl
from jax.experimental.pallas import tpu as pltpu
from jax.sharding import PartitionSpec as P

W = 36
X, Z_HI, Z_LO = 4, 2, 4
STEP_ROWS = 4
CHUNKS = 4
MESH = pl.DeviceIdType.MESH


def places():
    basis, state = lax.axis_index("basis"), lax.axis_index("state")
    inner = lax.axis_size("basis") // Z_LO
    x, z_hi = lax.div(state, Z_HI), lax.rem(state, Z_HI)
    z_lo, rest = lax.div(basis, inner), lax.rem(basis, inner)
    z = z_hi * Z_LO + z_lo

    def along_x(shift):
        return (basis, lax.rem(x + shift + X, X) * Z_HI + z_hi)

    def along_z(shift):
        moved = lax.rem(z + shift + Z_HI * Z_LO, Z_HI * Z_LO)
        return (lax.rem(moved, Z_LO) * inner + rest, x * Z_HI + lax.div(moved, Z_LO))

    return {
        "right": along_x(1),
        "left": along_x(-1),
        "ahead": along_z(2),
        "behind": along_z(-2),
    }


def greet(partners):
    barrier = pltpu.get_barrier_semaphore()
    for device in partners:
        pl.semaphore_signal(barrier, inc=1, device_id=device, device_id_type=MESH)
    pl.semaphore_wait(barrier, len(partners))


def sender(send_sems, recv_sems):
    used = iter(range(send_sems.shape[0]))

    def make(source, target, device):
        n = next(used)
        return pltpu.make_async_remote_copy(
            src_ref=source,
            dst_ref=target,
            send_sem=send_sems.at[n],
            recv_sem=recv_sems.at[n],
            device_id=device,
            device_id_type=MESH,
        )

    return make


def gather_kernel(vectors, mine, low, high, relay, send_sems, recv_sems):
    at = places()
    basis, state = lax.axis_index("basis"), lax.axis_index("state")
    devices = lax.axis_size("basis")
    up = (lax.rem(basis + 1, devices), state)
    down = (lax.rem(basis + devices - 1, devices), state)
    has_up, has_down = basis < devices - 1, basis > 0
    make = sender(send_sems, recv_sems)
    width, reach = vectors.shape[1], low.shape[2]
    cut = vectors.shape[0] // 2
    halves = (pl.ds(0, cut), pl.ds(cut, cut))

    greet([*at.values(), up, down])

    plain, edges = [], []

    def start(copy):
        copy.start()
        plain.append(copy)
        return copy

    def halo(piece, source):
        rising = make(source.at[:, pl.ds(width - reach, reach)], low.at[piece], up)
        falling = make(source.at[:, pl.ds(0, reach)], high.at[piece], down)

        @pl.when(has_up)
        def _():
            rising.start()

        @pl.when(has_down)
        def _():
            falling.start()

        edges.append((rising, falling))

    z_routes = ("ahead", "behind")
    first = [
        start(make(vectors.at[half], relay.at[half], at[route]))
        for half, route in zip(halves, z_routes)
    ]

    def spread(base, source):
        to_left = start(make(source, mine.at[base], at["left"]))
        to_right = start(make(source, mine.at[base + 1], at["right"]))
        halo(base, source)
        return to_left, to_right

    def forward(base, to_left, to_right):
        to_left.wait_recv()
        far = [start(make(mine.at[base, halves[0]], mine.at[base + 2, halves[0]], at["left"]))]
        halo(base + 1, mine.at[base])
        to_right.wait_recv()
        far.append(
            start(make(mine.at[base + 1, halves[1]], mine.at[base + 2, halves[1]], at["right"]))
        )
        halo(base + 2, mine.at[base + 1])
        return far

    own = spread(0, vectors)
    second = []
    for copy, half, route in zip(first, halves, z_routes):
        copy.wait_recv()
        second.append(start(make(relay.at[half], mine.at[3, half], at[route])))
    own_far = forward(0, *own)
    for copy in second:
        copy.wait_recv()
    other = spread(4, mine.at[3])
    for copy in own_far:
        copy.wait_recv()
    halo(3, mine.at[2])
    other_far = forward(4, *other)
    for copy in other_far:
        copy.wait_recv()
    halo(7, mine.at[6])

    for copy in plain:
        copy.wait_send()
    for rising, falling in edges:

        @pl.when(has_up)
        def _():
            rising.wait_send()
            falling.wait_recv()

        @pl.when(has_down)
        def _():
            falling.wait_send()
            rising.wait_recv()


def gather(vectors, size):
    states, width = vectors.shape
    reach = W * size
    copies = 2 + 2 + 2 * 4 + 8 * 2
    anywhere = pl.BlockSpec(memory_space=pl.ANY)
    return pl.pallas_call(
        gather_kernel,
        out_shape=[
            jax.ShapeDtypeStruct((7, states, width), vectors.dtype),
            jax.ShapeDtypeStruct((8, states, reach), vectors.dtype),
            jax.ShapeDtypeStruct((8, states, reach), vectors.dtype),
            jax.ShapeDtypeStruct((states, width), vectors.dtype),
        ],
        in_specs=[anywhere],
        out_specs=[anywhere] * 4,
        scratch_shapes=[
            pltpu.SemaphoreType.DMA((copies,)),
            pltpu.SemaphoreType.DMA((copies,)),
        ],
        compiler_params=pltpu.CompilerParams(collective_id=0, has_side_effects=True),
    )(vectors)[:3]


def product_kernel(slots, relative, live, blocks, vectors, mine, low, high, out, panel, sems):
    states, size = out.shape[1], blocks.shape[2]
    width, reach = vectors.shape[1], low.shape[2]

    @pl.when(pl.program_id(0) == 0)
    def _():
        copies = []
        for piece in range(8):
            rows = pl.ds(piece * states, states)
            middle = vectors if piece == 0 else mine.at[piece - 1]
            for source, start, length in (
                (low.at[piece], 0, reach),
                (middle, reach, width),
                (high.at[piece], reach + width, reach),
            ):
                copies.append(
                    pltpu.make_async_copy(
                        source, panel.at[rows, pl.ds(start, length)], sems.at[len(copies)]
                    )
                )
        for copy in copies:
            copy.start()
        for copy in copies:
            copy.wait()

    for row in range(STEP_ROWS):
        base = (pl.program_id(0) * STEP_ROWS + row) * slots
        total = None
        for first in range(0, slots, 2):
            group = range(first, min(first + 2, slots))
            picked = [
                panel[:, pl.ds(pl.multiple_of(relative[base + k] * size, size), size)] for k in group
            ]
            weight = [
                jnp.where(live[base + k] > 0, blocks[row, k], jnp.zeros_like(blocks[row, k]))
                for k in group
            ]
            term = lax.dot_general(
                jnp.concatenate(picked, axis=1),
                jnp.concatenate(weight, axis=1),
                (((1,), (1,)), ((), ())),
                preferred_element_type=jnp.float32,
            )
            total = term if total is None else total + term
        out[:, :, row * size : (row + 1) * size] = total.reshape(8, states, size)


def product(relative, live, blocks, vectors, mine, low, high):
    rows, slots, size, _ = blocks.shape
    states, width = vectors.shape
    anywhere = pl.BlockSpec(memory_space=pl.ANY)
    grid_spec = pltpu.PrefetchScalarGridSpec(
        num_scalar_prefetch=2,
        grid=(rows // STEP_ROWS,),
        in_specs=[
            pl.BlockSpec((STEP_ROWS, slots, size, size), lambda i, *_: (i, 0, 0, 0)),
        ]
        + [anywhere] * 4,
        out_specs=pl.BlockSpec((8, states, STEP_ROWS * size), lambda i, *_: (0, 0, i)),
        scratch_shapes=[
            pltpu.VMEM((8 * states, width + 2 * W * size), jnp.bfloat16),
            pltpu.SemaphoreType.DMA((24,)),
        ],
    )
    return pl.pallas_call(
        functools.partial(product_kernel, slots),
        grid_spec=grid_spec,
        out_shape=jax.ShapeDtypeStruct((8, states, width), jnp.float32),
        compiler_params=pltpu.CompilerParams(vmem_limit_bytes=40 * 1024 * 1024),
    )(relative, live, blocks, vectors, mine, low, high)


def reduce_kernel(partial, out, passing, joined, direct, relay, away, send_sems, recv_sems):
    at = places()
    greet(list(at.values()))
    make = sender(send_sems, recv_sems)
    chunk = partial.shape[2] // CHUNKS
    started = []

    def start(source, target, device):
        copy = make(source, target, device)
        copy.start()
        started.append(copy)
        return copy

    def part(z, piece, q):
        return partial.at[z * 4 + piece, :, pl.ds(q * chunk, chunk)]

    units = [(z, q) for z in (1, 0) for q in range(CHUNKS)]
    index = {unit: n for n, unit in enumerate(units)}
    ways = (("right", "left", 1, 2), ("left", "right", 2, 1))
    far, near, joint, hop, final = {}, {}, {}, {}, {}

    def send(unit):
        z, q = unit
        to, back, _, plain = ways[q % 2]
        n = index[unit]
        far[unit] = start(part(z, 3, q), passing.at[n], at[to])
        near[unit] = start(part(z, plain, q), direct.at[n], at[back])

    def join(unit):
        z, q = unit
        to, _, piece, _ = ways[q % 2]
        n = index[unit]
        far[unit].wait_recv()
        passing[n] = part(z, piece, q)[...] + passing[n]
        joint[unit] = start(passing.at[n], joined.at[n], at[to])

    def finish(unit):
        z, q = unit
        n = index[unit]
        joint[unit].wait_recv()
        near[unit].wait_recv()
        joined[n] = part(z, 0, q)[...] + joined[n] + direct[n]
        if z == 1:
            route = at["ahead" if q % 2 == 0 else "behind"]
            hop[q] = start(joined.at[n], relay.at[q], route)

    def pass_on(q):
        hop[q].wait_recv()
        route = at["ahead" if q % 2 == 0 else "behind"]
        final[q] = start(relay.at[q], away.at[q], route)

    pairs = [units[i : i + 2] for i in range(0, len(units), 2)]
    half = CHUNKS // 2
    for unit in pairs[0]:
        send(unit)
    for n, pair in enumerate(pairs):
        if n + 1 < len(pairs):
            for unit in pairs[n + 1]:
                send(unit)
        for unit in pair:
            join(unit)
        if n >= 1:
            for unit in pairs[n - 1]:
                finish(unit)
        if 2 <= n < 2 + half:
            for unit in pairs[n - 2]:
                pass_on(unit[1])
    for unit in pairs[-1]:
        finish(unit)
    for q in range(CHUNKS):
        if q not in final:
            pass_on(q)
    for q in range(CHUNKS):
        final[q].wait_recv()
        columns = pl.ds(q * chunk, chunk)
        out[:, columns] = (joined[index[(0, q)]] + away[q]).astype(out.dtype)
    for copy in started:
        copy.wait_send()


def reduce(partial):
    _, states, width = partial.shape
    chunk = width // CHUNKS
    copies = 2 * CHUNKS * 3 + CHUNKS * 2
    in_vmem = pl.BlockSpec(memory_space=pltpu.VMEM)
    slots = pltpu.VMEM((2 * CHUNKS, states, chunk), jnp.float32)
    return pl.pallas_call(
        reduce_kernel,
        out_shape=jax.ShapeDtypeStruct((states, width), jnp.bfloat16),
        in_specs=[in_vmem],
        out_specs=in_vmem,
        scratch_shapes=[
            slots,
            slots,
            slots,
            pltpu.VMEM((CHUNKS, states, chunk), jnp.float32),
            pltpu.VMEM((CHUNKS, states, chunk), jnp.float32),
            pltpu.SemaphoreType.DMA((copies,)),
            pltpu.SemaphoreType.DMA((copies,)),
        ],
        compiler_params=pltpu.CompilerParams(
            collective_id=1, has_side_effects=True, vmem_limit_bytes=40 * 1024 * 1024
        ),
    )(partial)


def on_device(vectors, blocks, columns, counts):
    rows, slots, size, _ = blocks.shape
    first_block = lax.axis_index("basis") * rows - W
    relative = (columns - first_block).reshape(-1)
    slot_index = lax.axis_index("state") * slots + jnp.arange(slots, dtype=jnp.int32)
    live = (slot_index[None, :] < counts[:, None]).astype(jnp.int32).reshape(-1)
    mine, low, high = gather(vectors, size)
    return reduce(product(relative, live, blocks, vectors, mine, low, high))


def solution(mesh):
    in_specs = (
        P("state", "basis"),
        P("basis", "state", None, None),
        P("basis", "state"),
        P("basis"),
    )
    out_specs = P("state", "basis")
    return jax.shard_map(
        on_device, mesh=mesh, in_specs=in_specs, out_specs=out_specs, check_vma=False
    )
```

time: 625 us -> 219 us (0.35)
  waiting for transfers between devices: 494 us -> 0 us
  Pallas kernels: 0 us -> 202 us
  local copies, waits for them, and re-layouts: 76.8 us -> 10.8 us
  matrix products: 26.1 us -> 0 us
  between operations: 13.5 us -> 0.05 us
    all_gather x1 -> x0, waiting for transfers between devices: 273 us -> none  [on_device(): gathered = lax.all_gather(banded, 'state', axis=0, tiled=True)]
    reduce_scatter x1 -> x0, waiting for transfers between devices: 210 us -> none  [on_device(): lax.psum_scatter(result.reshape(row_count, shard_rows), 'state', scatter_...]
    pallas_call x0 -> x3, Pallas kernels: none -> 202 us  [the longest x1 94.2 us: reduce(): pl.pallas_call(reduce_kernel, out_shape=jax.ShapeDtypeStruct((states, wid...]
    reshape x2 -> x0, local copies, waits for them, and re-layouts: 31.4 us -> none  [the longest x1 19.9 us: on_device(): state_part = state_part.reshape(row_count, row_blocks + 2 * W, block_size)]
    dot_general x1 -> x0, matrix products: 26.1 us -> none  [on_device(): jnp.einsum('srjb,rjcb->src', picked, blocks, preferred_element_type=jnp.f...]
    gather x1 -> x0, local copies, waits for them, and re-layouts: 23.8 us -> none  [on_device(): jnp.take(state_part, relative, axis=1)]
    all_gather x1 -> x0, local copies, waits for them, and re-layouts: 20 us -> none  [on_device(): gathered = lax.all_gather(banded, 'state', axis=0, tiled=True)]
    ppermute x2 -> x0, waiting for transfers between devices: 11.4 us -> none  [the longest x1 6.51 us: extended(): after = lax.ppermute(leading, axis, down)]
  transfers between devices with their start and end apart: 4 -> 0, of which waited for: 4 -> 0; matrix products, arithmetic and copies ran while one was open for 0% -> 0% of each run, Pallas kernels for 0% -> 0%
where the time goes in v2:
time: 219 us; the launch traced here: 215 us
  Pallas kernels  202 us (92%)
  local copies, waits for them, and re-layouts  10.8 us (5%)
    pallas_call x1, Pallas kernels, reduce(): pl.pallas_call(reduce_kernel, out_shape=jax.ShapeDtypeStruct((states, wid...  94.2 us
    pallas_call x1, Pallas kernels, gather(): pl.pallas_call(gather_kernel, out_shape=[jax.ShapeDtypeStruct((7, states,...  87 us
    pallas_call x1, Pallas kernels, product(): pl.pallas_call(functools.partial(product_kernel, slots), grid_spec=grid_s...  21.2 us
    unnamed x9, local copies, waits for them, and re-layouts  10.5 us

profile of v2, /device:TPU:25, one launch (start us, length us, event | category | flops | bytes accessed | tf_op | source)
XLA Modules:
  0.0 214.8 jit_solution(14602283055557583222)
XLA Ops:
  0.0 0.7 broadcast_subtract_fusion
  0.7 0.1 copy.5
  0.8 0.1 reshape.14.relative
  0.9 0.7 compare_convert_fusion
  1.6 0.1 reshape.15.live
  1.8 87.0 %shard_map.46 = (bf16[7,64,5120]{2,1,0:T(8,128)(2,1)}, bf16[8,64,4608]{2,1,0:T(8,128)(2,1)}, bf16[8,64,4608]{2,1,0:T(8,128)(2,1)}, bf16[64,5120]{1,0:T(8,128)(2,1)}) custom-call(bf16[64,5120]{1,0:T(8,128)(2,1)} %vectors.3), custom_call_target="tpu_custom_call" | custom-call | tf_op jit(solution)/shard_map/pallas_call | solution.py:158
  88.8 0.0 copy-start.1
  88.8 2.3 %copy-done.1 = bf16[8,64,4608]{2,1,0:T(8,128)(2,1)S(1)} copy-done((bf16[8,64,4608]{2,1,0:T(8,128)(2,1)S(1)}, bf16[8,64,4608]{2,1,0:T(8,128)(2,1)}, u32[]{:S(2)}) %copy-start.1) | copy-done | bytes 4718616
  91.1 0.0 copy-start.2
  91.1 2.3 %copy-done.2 = bf16[7,64,5120]{2,1,0:T(8,128)(2,1)S(1)} copy-done((bf16[7,64,5120]{2,1,0:T(8,128)(2,1)S(1)}, bf16[7,64,5120]{2,1,0:T(8,128)(2,1)}, u32[]{:S(2)}) %copy-start.2) | copy-done | bytes 4587544
  93.4 0.0 copy-start.3
  93.4 1.1 copy-done.3
  94.5 21.2 %shard_map.47.partial = f32[8,64,5120]{2,1,0:T(8,128)} custom-call(s32[360]{0:T(512)S(1)} %reshape.14.relative, s32[360]{0:T(512)S(1)} %reshape.15.live, bf16[40,9,128,128]{3,2,1,0:T(8,128)(2,1)} %blocks.1, bf16[64,5120]{1,0:T(8,128)(2,1)S(1)} %copy-done.3, bf16[7,64,5120]{2,1,0:T(8,128)(2,1)S(1)} %copy-done.2, bf16[8,64,4608]{2,1,0:T(8,128)(2,1)S(1)} %copy-done.1, ...), custom_call_target="tpu_custom_call" | custom-call | tf_op jit(solution)/shard_map/pallas_call | solution.py:240
  115.7 0.0 copy-start
  115.7 4.0 %copy-done = f32[8,64,5120]{2,1,0:T(8,128)S(1)} copy-done((f32[8,64,5120]{2,1,0:T(8,128)S(1)}, f32[8,64,5120]{2,1,0:T(8,128)}, u32[]{:S(2)}) %copy-start) | copy-done | bytes 10485784
  119.7 94.2 %shard_map.48 = bf16[64,5120]{1,0:T(8,128)(2,1)S(1)} custom-call(f32[8,64,5120]{2,1,0:T(8,128)S(1)} %copy-done), custom_call_target="tpu_custom_call" | custom-call | tf_op jit(solution)/shard_map/pallas_call | solution.py:334
  213.9 0.8 copy.7
  (1 shorter events, 0.0 us)
Async XLA Ops:
  88.8 2.3 %copy-start.1 = (bf16[8,64,4608]{2,1,0:T(8,128)(2,1)S(1)}, bf16[8,64,4608]{2,1,0:T(8,128)(2,1)}, u32[]{:S(2)}) copy-start(bf16[8,64,4608]{2,1,0:T(8,128)(2,1)} %get-tuple-element.9.low) | copy-start | bytes 14155780
  91.1 2.3 %copy-start.2 = (bf16[7,64,5120]{2,1,0:T(8,128)(2,1)S(1)}, bf16[7,64,5120]{2,1,0:T(8,128)(2,1)}, u32[]{:S(2)}) copy-start(bf16[7,64,5120]{2,1,0:T(8,128)(2,1)} %get-tuple-element.8.mine) | copy-start | bytes 13762564
  93.4 1.1 copy-start.3
  115.7 4.0 %copy-start = (f32[8,64,5120]{2,1,0:T(8,128)S(1)}, f32[8,64,5120]{2,1,0:T(8,128)}, u32[]{:S(2)}) copy-start(f32[8,64,5120]{2,1,0:T(8,128)} %shard_map.47.partial) | copy-start | bytes 31457284

commit v3 on v0

v3 whole, which is shorter than its diff:
```python
import jax
import jax.numpy as jnp
from jax import lax
from jax.experimental import pallas as pl
from jax.experimental.pallas import tpu as pltpu
from jax.sharding import PartitionSpec as P

W = 36
X, Z_HI, Z_LO = 4, 2, 4
CHUNKS = 4
MESH = pl.DeviceIdType.MESH


def places():
    basis, state = lax.axis_index("basis"), lax.axis_index("state")
    inner = lax.axis_size("basis") // Z_LO
    x, z_hi = lax.div(state, Z_HI), lax.rem(state, Z_HI)
    z_lo, rest = lax.div(basis, inner), lax.rem(basis, inner)
    z = z_hi * Z_LO + z_lo

    def along_x(shift):
        return (basis, lax.rem(x + shift + X, X) * Z_HI + z_hi)

    def along_z(shift):
        moved = lax.rem(z + shift + Z_HI * Z_LO, Z_HI * Z_LO)
        return (lax.rem(moved, Z_LO) * inner + rest, x * Z_HI + lax.div(moved, Z_LO))

    return {
        "right": along_x(1),
        "left": along_x(-1),
        "ahead": along_z(2),
        "behind": along_z(-2),
    }


def greet(partners):
    barrier = pltpu.get_barrier_semaphore()
    for device in partners:
        pl.semaphore_signal(barrier, inc=1, device_id=device, device_id_type=MESH)
    pl.semaphore_wait(barrier, len(partners))


def sender(send_sems, recv_sems):
    used = iter(range(send_sems.shape[0]))

    def make(source, target, device):
        n = next(used)
        return pltpu.make_async_remote_copy(
            src_ref=source,
            dst_ref=target,
            send_sem=send_sems.at[n],
            recv_sem=recv_sems.at[n],
            device_id=device,
            device_id_type=MESH,
        )

    return make


def sigma_kernel(
    relative, live, vectors, blocks, out,
    own_panel, other_panel, held, relay, partial, passing, joined, direct, hopping, away,
    send_sems, recv_sems, local_sems,
):
    at = places()
    basis, state = lax.axis_index("basis"), lax.axis_index("state")
    devices = lax.axis_size("basis")
    up = (lax.rem(basis + 1, devices), state)
    down = (lax.rem(basis + devices - 1, devices), state)
    has_up, has_down = basis < devices - 1, basis > 0
    make = sender(send_sems, recv_sems)
    states = vectors.shape[1]
    rows, slots, size, _ = blocks.shape
    width = rows * size
    cut = states // 2
    halves = (pl.ds(0, cut), pl.ds(cut, cut))
    panels = (own_panel, other_panel)
    z_routes = ("ahead", "behind")

    greet([*at.values(), up, down])
    started, edges = [], {}

    def start(source, target, device):
        copy = make(source, target, device)
        copy.start()
        started.append(copy)
        return copy

    def middle(z, piece, first=0, count=states):
        return panels[z].at[pl.ds(W, rows), pl.ds(piece * states + first, count)]

    def halo(z, piece, source):
        lines = pl.ds(piece * states, states)
        low = panels[z].at[pl.ds(0, W), lines]
        high = panels[z].at[pl.ds(W + rows, W), lines]
        rising = make(source.at[pl.ds(rows - W, W)], low, up)
        falling = make(source.at[pl.ds(0, W)], high, down)

        @pl.when(has_up)
        def _():
            rising.start()

        @pl.when(has_down)
        def _():
            falling.start()

        edges[z, piece] = (rising, falling)

    def spread(z, source):
        to_left = start(source, middle(z, 1), at["left"])
        to_right = start(source, middle(z, 2), at["right"])
        halo(z, 0, source)
        return to_left, to_right

    def forward(z, to_left, to_right):
        to_left.wait_recv()
        far = [start(middle(z, 1, 0, cut), middle(z, 3, 0, cut), at["left"])]
        halo(z, 1, middle(z, 1))
        to_right.wait_recv()
        far.append(start(middle(z, 2, cut, cut), middle(z, 3, cut, cut), at["right"]))
        halo(z, 2, middle(z, 2))
        return far

    def edges_arrived(z):
        for piece in range(4):
            rising, falling = edges[z, piece]

            @pl.when(has_up)
            def _():
                falling.wait_recv()

            @pl.when(has_down)
            def _():
                rising.wait_recv()

    first = [
        start(vectors.at[:, half], relay.at[:, half], at[route])
        for half, route in zip(halves, z_routes)
    ]
    own = spread(0, vectors)
    local = [
        pltpu.make_async_copy(vectors, middle(0, 0), local_sems.at[0]),
        pltpu.make_async_copy(blocks, held, local_sems.at[1]),
    ]
    for copy in local:
        copy.start()
    second = []
    for n, (copy, route) in enumerate(zip(first, z_routes)):
        copy.wait_recv()
        second.append(start(relay.at[:, halves[n]], middle(1, 0, n * cut, cut), at[route]))
    own_far = forward(0, *own)
    for copy in second:
        copy.wait_recv()
    other = spread(1, middle(1, 0))
    for copy in own_far:
        copy.wait_recv()
    halo(0, 3, middle(0, 3))
    other_far = forward(1, *other)
    for copy in other_far:
        copy.wait_recv()
    halo(1, 3, middle(1, 3))
    for copy in local:
        copy.wait()

    chunk = width // CHUNKS
    units = [(z, q) for z in (0, 1) for q in range(CHUNKS)]
    index = {unit: n for n, unit in enumerate(units)}
    ways = (("right", "left", 1, 2), ("left", "right", 2, 1))
    far, near, joint, hop, final = {}, {}, {}, {}, {}

    def part(n, piece):
        return partial.at[n, pl.ds(piece * states, states)]

    def multiply(unit):
        z, q = unit
        n = index[unit]
        panel = panels[z]

        def one_row(i, carry):
            row = q * (rows // CHUNKS) + i
            base = row * slots
            total = None
            for first in range(0, slots, 2):
                group = range(first, min(first + 2, slots))
                picked = [panel[relative[base + k]] for k in group]
                weight = [
                    held[row, k] * jnp.full((size, size), live[base + k]).astype(held.dtype)
                    for k in group
                ]
                term = lax.dot_general(
                    jnp.concatenate(picked, axis=1),
                    jnp.concatenate(weight, axis=1),
                    (((1,), (1,)), ((), ())),
                    preferred_element_type=jnp.float32,
                )
                total = term if total is None else total + term
            partial[n, :, pl.ds(pl.multiple_of(i * size, size), size)] = total
            return carry

        lax.fori_loop(0, rows // CHUNKS, one_row, 0)

    def send(unit):
        multiply(unit)
        to, back, _, plain = ways[unit[1] % 2]
        n = index[unit]
        far[unit] = start(part(n, 3), passing.at[n], at[to])
        near[unit] = start(part(n, plain), direct.at[n], at[back])

    def join(unit):
        to, _, piece, _ = ways[unit[1] % 2]
        n = index[unit]
        far[unit].wait_recv()
        passing[n] = part(n, piece)[...] + passing[n]
        joint[unit] = start(passing.at[n], joined.at[n], at[to])

    def finish(unit):
        z, q = unit
        n = index[unit]
        joint[unit].wait_recv()
        near[unit].wait_recv()
        joined[n] = part(n, 0)[...] + joined[n] + direct[n]
        if z == 1:
            hop[q] = start(joined.at[n], hopping.at[q], at[z_routes[q % 2]])

    def pass_on(unit):
        q = unit[1]
        hop[q].wait_recv()
        final[q] = start(hopping.at[q], away.at[q], at[z_routes[q % 2]])

    pairs = [units[i : i + 2] for i in range(0, len(units), 2)]

    def each(step, n):
        for unit in pairs[n]:
            step(unit)

    edges_arrived(0)
    each(send, 0)
    each(send, 1)
    each(join, 0)
    edges_arrived(1)
    each(send, 2)
    each(join, 1)
    each(send, 3)
    each(join, 2)
    each(finish, 0)
    each(join, 3)
    each(finish, 1)
    each(finish, 2)
    each(pass_on, 2)
    each(finish, 3)
    each(pass_on, 3)
    for q in range(CHUNKS):
        final[q].wait_recv()
        out[:, pl.ds(q * chunk, chunk)] = (joined[index[0, q]] + away[q]).astype(out.dtype)

    for copy in started:
        copy.wait_send()
    for rising, falling in edges.values():

        @pl.when(has_up)
        def _():
            rising.wait_send()

        @pl.when(has_down)
        def _():
            falling.wait_send()


def sigma(relative, live, vectors, blocks):
    rows, slots, size, _ = blocks.shape
    states, width = vectors.shape[1], rows * size
    chunk = width // CHUNKS
    copies = 2 + 2 + 2 * 4 + 8 * 2 + 2 * CHUNKS * 3 + CHUNKS * 2
    panel = pltpu.VMEM((rows + 2 * W, 4 * states, size), vectors.dtype)
    all_units = pltpu.VMEM((2 * CHUNKS, states, chunk), jnp.float32)
    half_units = pltpu.VMEM((CHUNKS, states, chunk), jnp.float32)
    return pl.pallas_call(
        sigma_kernel,
        out_shape=jax.ShapeDtypeStruct((states, width), jnp.bfloat16),
        in_specs=[pl.BlockSpec(memory_space=pltpu.SMEM)] * 2
        + [pl.BlockSpec(memory_space=pl.ANY)] * 2,
        out_specs=pl.BlockSpec(memory_space=pltpu.VMEM),
        scratch_shapes=[
            panel,
            panel,
            pltpu.VMEM(blocks.shape, blocks.dtype),
            pltpu.VMEM(vectors.shape, vectors.dtype),
            pltpu.VMEM((2 * CHUNKS, 4 * states, chunk), jnp.float32),
            all_units,
            all_units,
            all_units,
            half_units,
            half_units,
            pltpu.SemaphoreType.DMA((copies,)),
            pltpu.SemaphoreType.DMA((copies,)),
            pltpu.SemaphoreType.DMA((2,)),
        ],
        compiler_params=pltpu.CompilerParams(
            collective_id=0, has_side_effects=True, vmem_limit_bytes=60 * 1024 * 1024
        ),
    )(relative, live, vectors, blocks)


def on_device(vectors, blocks, columns, counts):
    rows, slots, size, _ = blocks.shape
    first_block = lax.axis_index("basis") * rows - W
    relative = (columns - first_block).reshape(-1)
    slot_index = lax.axis_index("state") * slots + jnp.arange(slots, dtype=jnp.int32)
    live = (slot_index[None, :] < counts[:, None]).astype(jnp.float32).reshape(-1)
    by_block = jnp.transpose(vectors.reshape(-1, rows, size), (1, 0, 2))
    return sigma(relative, live, by_block, blocks)


def solution(mesh):
    in_specs = (
        P("state", "basis"),
        P("basis", "state", None, None),
        P("basis", "state"),
        P("basis"),
    )
    out_specs = P("state", "basis")
    return jax.shard_map(
        on_device, mesh=mesh, in_specs=in_specs, out_specs=out_specs, check_vma=False
    )
```

time: 625 us -> 219 us (0.35)
  waiting for transfers between devices: 494 us -> 0 us
  Pallas kernels: 0 us -> 213 us
  local copies, waits for them, and re-layouts: 76.8 us -> 4.46 us
  matrix products: 26.1 us -> 0 us
  between operations: 13.5 us -> 0.02 us
    all_gather x1 -> x0, waiting for transfers between devices: 273 us -> none  [on_device(): gathered = lax.all_gather(banded, 'state', axis=0, tiled=True)]
    pallas_call x0 -> x1, Pallas kernels: none -> 213 us  [sigma(): pl.pallas_call(sigma_kernel, out_shape=jax.ShapeDtypeStruct((states, widt...]
    reduce_scatter x1 -> x0, waiting for transfers between devices: 210 us -> none  [on_device(): lax.psum_scatter(result.reshape(row_count, shard_rows), 'state', scatter_...]
    reshape x2 -> x0, local copies, waits for them, and re-layouts: 31.4 us -> none  [the longest x1 19.9 us: on_device(): state_part = state_part.reshape(row_count, row_blocks + 2 * W, block_size)]
    dot_general x1 -> x0, matrix products: 26.1 us -> none  [on_device(): jnp.einsum('srjb,rjcb->src', picked, blocks, preferred_element_type=jnp.f...]
    gather x1 -> x0, local copies, waits for them, and re-layouts: 23.8 us -> none  [on_device(): jnp.take(state_part, relative, axis=1)]
    all_gather x1 -> x0, local copies, waits for them, and re-layouts: 20 us -> none  [on_device(): gathered = lax.all_gather(banded, 'state', axis=0, tiled=True)]
    ppermute x2 -> x0, waiting for transfers between devices: 11.4 us -> none  [the longest x1 6.51 us: extended(): after = lax.ppermute(leading, axis, down)]
  transfers between devices with their start and end apart: 4 -> 0, of which waited for: 4 -> 0; matrix products, arithmetic and copies ran while one was open for 0% -> 0% of each run, Pallas kernels for 0% -> 0%
where the time goes in v3:
time: 219 us
  Pallas kernels  213 us (97%)
  local copies, waits for them, and re-layouts  4.46 us (2%)
    pallas_call x1, Pallas kernels, sigma(): pl.pallas_call(sigma_kernel, out_shape=jax.ShapeDtypeStruct((states, widt...  213 us

profile of v3, /device:TPU:25, one launch (start us, length us, event | category | flops | bytes accessed | tf_op | source)
XLA Modules:
  0.0 219.0 jit_solution(13491638106397919291)
XLA Ops:
  0.0 0.0 copy-start
  0.0 0.8 broadcast_subtract_fusion
  0.8 0.1 copy.5
  0.9 0.7 reshape.17.relative
  1.6 0.7 compare_convert_fusion
  2.3 0.7 reshape.19.live
  3.0 0.0 copy-done
  3.0 1.0 bitcast_bitcast_fusion.vectors
  4.0 213.0 %shard_map.46 = bf16[64,5120]{1,0:T(8,128)(2,1)} custom-call(s32[360]{0:T(512)} %reshape.17.relative, f32[360]{0:T(512)} %reshape.19.live, bf16[40,64,128]{2,1,0:T(8,128)(2,1)} %bitcast_bitcast_fusion.vectors, bf16[40,9,128,128]{3,2,1,0:T(8,128)(2,1)} %blocks.1), custom_call_target="tpu_custom_call" | custom-call | tf_op jit(solution)/shard_map/pallas_call | solution.py:277
  217.0 2.0 copy.10
  (1 shorter events, 0.0 us)
Async XLA Ops:
  0.0 3.0 %copy-start = (bf16[64,5120]{1,0:T(8,128)(2,1)S(1)}, bf16[64,5120]{1,0:T(8,128)(2,1)}, u32[]{:S(2)}) copy-start(bf16[64,5120]{1,0:T(8,128)(2,1)} %param.4) | copy-start | bytes 1966084

commit v4 on v3

--- a/solution.py
+++ b/solution.py
@@ -7,7 +7,7 @@
 
 W = 36
 X, Z_HI, Z_LO = 4, 2, 4
-CHUNKS = 4
+CHUNKS = 8
 MESH = pl.DeviceIdType.MESH
 
 
@@ -200,7 +200,6 @@
         lax.fori_loop(0, rows // CHUNKS, one_row, 0)
 
     def send(unit):
-        multiply(unit)
         to, back, _, plain = ways[unit[1] % 2]
         n = index[unit]
         far[unit] = start(part(n, 3), passing.at[n], at[to])
@@ -233,22 +232,42 @@
         for unit in pairs[n]:
             step(unit)
 
+    def feed(unit):
+        multiply(unit)
+        send(unit)
+
     edges_arrived(0)
-    each(send, 0)
-    each(send, 1)
+    each(feed, 0)
+    each(feed, 1)
     each(join, 0)
+    each(multiply, 2)
+    each(multiply, 3)
+    each(join, 1)
     edges_arrived(1)
+    each(feed, 4)
+    each(feed, 5)
+    each(join, 4)
+    each(feed, 6)
+    each(join, 5)
+    each(feed, 7)
+    each(finish, 4)
+    each(join, 6)
+    each(finish, 5)
+    each(pass_on, 4)
+    each(join, 7)
     each(send, 2)
-    each(join, 1)
     each(send, 3)
+    each(finish, 6)
+    each(pass_on, 5)
+    each(finish, 7)
+    each(pass_on, 6)
     each(join, 2)
+    each(join, 3)
     each(finish, 0)
-    each(join, 3)
     each(finish, 1)
+    each(pass_on, 7)
     each(finish, 2)
-    each(pass_on, 2)
     each(finish, 3)
-    each(pass_on, 3)
     for q in range(CHUNKS):
         final[q].wait_recv()
         out[:, pl.ds(q * chunk, chunk)] = (joined[index[0, q]] + away[q]).astype(out.dtype)

time: 219 us -> 178 us (0.81)
  Pallas kernels: 213 us -> 171 us
    pallas_call x1, Pallas kernels: 213 us -> 171 us  [sigma(): pl.pallas_call(sigma_kernel, out_shape=jax.ShapeDtypeStruct((states, widt...]
where the time goes in v4:
time: 178 us; the launch traced here: 177 us
  Pallas kernels  171 us (96%)
  local copies, waits for them, and re-layouts  4.46 us (3%)
    pallas_call x1, Pallas kernels, sigma(): pl.pallas_call(sigma_kernel, out_shape=jax.ShapeDtypeStruct((states, widt...  171 us

profile of v4, /device:TPU:25, one launch (start us, length us, event | category | flops | bytes accessed | tf_op | source)
XLA Modules:
  0.0 177.2 jit_solution(2570938600882979834)
XLA Ops:
  0.0 0.0 copy-start
  0.0 0.8 broadcast_subtract_fusion
  0.8 0.1 copy.5
  0.9 0.7 reshape.17.relative
  1.6 0.7 compare_convert_fusion
  2.3 0.7 reshape.19.live
  3.0 0.0 copy-done
  3.0 1.0 bitcast_bitcast_fusion.vectors
  4.0 171.2 %shard_map.46 = bf16[64,5120]{1,0:T(8,128)(2,1)} custom-call(s32[360]{0:T(512)} %reshape.17.relative, f32[360]{0:T(512)} %reshape.19.live, bf16[40,64,128]{2,1,0:T(8,128)(2,1)} %bitcast_bitcast_fusion.vectors, bf16[40,9,128,128]{3,2,1,0:T(8,128)(2,1)} %blocks.1), custom_call_target="tpu_custom_call" | custom-call | tf_op jit(solution)/shard_map/pallas_call | solution.py:296
  175.2 2.0 %copy.10 = bf16[64,5120]{1,0:T(8,128)(2,1)} copy(bf16[64,5120]{1,0:T(8,128)(2,1)} %shard_map.46) | data formatting | bytes 1310720
  (1 shorter events, 0.0 us)
Async XLA Ops:
  0.0 3.0 %copy-start = (bf16[64,5120]{1,0:T(8,128)(2,1)S(1)}, bf16[64,5120]{1,0:T(8,128)(2,1)}, u32[]{:S(2)}) copy-start(bf16[64,5120]{1,0:T(8,128)(2,1)} %param.4) | copy-start | bytes 1966084

commit v5 on v4

--- a/solution.py
+++ b/solution.py
@@ -73,7 +73,8 @@
     rows, slots, size, _ = blocks.shape
     width = rows * size
     cut = states // 2
-    halves = (pl.ds(0, cut), pl.ds(cut, cut))
+    fine = cut // 2
+    legs = ((0, "ahead"), (cut, "behind"), (fine, "ahead"), (cut + fine, "behind"))
     panels = (own_panel, other_panel)
     z_routes = ("ahead", "behind")
 
@@ -134,8 +135,8 @@
                 rising.wait_recv()
 
     first = [
-        start(vectors.at[:, half], relay.at[:, half], at[route])
-        for half, route in zip(halves, z_routes)
+        start(vectors.at[:, pl.ds(line, fine)], relay.at[:, pl.ds(line, fine)], at[route])
+        for line, route in legs
     ]
     own = spread(0, vectors)
     local = [
@@ -145,9 +146,11 @@
     for copy in local:
         copy.start()
     second = []
-    for n, (copy, route) in enumerate(zip(first, z_routes)):
+    for copy, (line, route) in zip(first, legs):
         copy.wait_recv()
-        second.append(start(relay.at[:, halves[n]], middle(1, 0, n * cut, cut), at[route]))
+        second.append(
+            start(relay.at[:, pl.ds(line, fine)], middle(1, 0, line, fine), at[route])
+        )
     own_far = forward(0, *own)
     for copy in second:
         copy.wait_recv()
@@ -289,7 +292,7 @@
     rows, slots, size, _ = blocks.shape
     states, width = vectors.shape[1], rows * size
     chunk = width // CHUNKS
-    copies = 2 + 2 + 2 * 4 + 8 * 2 + 2 * CHUNKS * 3 + CHUNKS * 2
+    copies = 4 + 4 + 2 * 4 + 8 * 2 + 2 * CHUNKS * 3 + CHUNKS * 2
     panel = pltpu.VMEM((rows + 2 * W, 4 * states, size), vectors.dtype)
     all_units = pltpu.VMEM((2 * CHUNKS, states, chunk), jnp.float32)
     half_units = pltpu.VMEM((CHUNKS, states, chunk), jnp.float32)

time: 178 us -> 175 us (0.983)
  Pallas kernels: 171 us -> 169 us
    pallas_call x1, Pallas kernels: 171 us -> 169 us  [sigma(): pl.pallas_call(sigma_kernel, out_shape=jax.ShapeDtypeStruct((states, widt...]
where the time goes in v5:
time: 175 us
  Pallas kernels  169 us (97%)
  local copies, waits for them, and re-layouts  4.46 us (3%)
    pallas_call x1, Pallas kernels, sigma(): pl.pallas_call(sigma_kernel, out_shape=jax.ShapeDtypeStruct((states, widt...  169 us

profile of v5, /device:TPU:25, one launch (start us, length us, event | category | flops | bytes accessed | tf_op | source)
XLA Modules:
  0.0 175.1 jit_solution(2700374673556772542)
XLA Ops:
  0.0 0.0 copy-start
  0.0 0.8 broadcast_subtract_fusion
  0.8 0.1 copy.5
  0.9 0.7 reshape.17.relative
  1.6 0.7 compare_convert_fusion
  2.3 0.7 reshape.19.live
  3.0 0.0 copy-done
  3.0 1.0 bitcast_bitcast_fusion.vectors
  4.0 169.1 %shard_map.46 = bf16[64,5120]{1,0:T(8,128)(2,1)} custom-call(s32[360]{0:T(512)} %reshape.17.relative, f32[360]{0:T(512)} %reshape.19.live, bf16[40,64,128]{2,1,0:T(8,128)(2,1)} %bitcast_bitcast_fusion.vectors, bf16[40,9,128,128]{3,2,1,0:T(8,128)(2,1)} %blocks.1), custom_call_target="tpu_custom_call" | custom-call | tf_op jit(solution)/shard_map/pallas_call | solution.py:299
  173.1 2.0 %copy.10 = bf16[64,5120]{1,0:T(8,128)(2,1)} copy(bf16[64,5120]{1,0:T(8,128)(2,1)} %shard_map.46) | data formatting | bytes 1310720
  (1 shorter events, 0.0 us)
Async XLA Ops:
  0.0 3.0 %copy-start = (bf16[64,5120]{1,0:T(8,128)(2,1)S(1)}, bf16[64,5120]{1,0:T(8,128)(2,1)}, u32[]{:S(2)}) copy-start(bf16[64,5120]{1,0:T(8,128)(2,1)} %param.4) | copy-start | bytes 1966084
